TPU v7x, 256 devices: a whole 4x4x8 slice. The times are simulated.
256 devices in a mesh: dp: 2 (over y_hi), expert: 128 (over x, y_lo, z, core).
Axes of the slice: x: 4, y: 4 (y_hi: 2, y_lo: 2; y = y_hi * 2 + y_lo), z: 8, core: 2. Of those that a mesh axis runs over, the one named last changes fastest.
Arguments:
- tokens: bfloat16 [4096, 4096], P(('dp', 'expert')), may hold values from -6 to 6
- routing: int32 [4096, 2], P(('dp', 'expert')), may hold values from 0 to 7, as said below
- hidden_grad: bfloat16 [131072, 512], P(('dp', 'expert')), may hold values from -3 to 3
- gate_weight: bfloat16 [4096, 65536], P(None, 'expert'), may hold values from -0.09375 to 0.09375
- up_weight: bfloat16 [4096, 65536], P(None, 'expert'), may hold values from -0.09375 to 0.09375
Outputs:
- token_grad: bfloat16 [4096, 4096], P(('dp', 'expert'))
- gate_weight_grad: bfloat16 [4096, 65536], P('dp', 'expert')
- up_weight_grad: bfloat16 [4096, 65536], P('dp', 'expert')
Inputs may be any that keep to these rules, and one draw needn't show every extreme that they name: `routing`: the 2 entries of a token differ, and no device names one expert in more than 4 of its tokens.
All inputs are finite; a program needn't handle non-finite values.
Results may differ from a plain program's by a relative error of at most 0.0085.
Values may be sent and summed in bfloat16 or wider, within the bound.
No kernel may reach another device: no remote copies, remote signals or barrier semaphores. Data moves between devices by JAX's collectives and lax.ppermute only.
A program may use at most 128 MiB of HBM per device.

v0:
```python
import jax
import jax.numpy as jnp
from jax import lax
from jax.sharding import PartitionSpec as P

EXPERTS = 8
TOP = 2
CAP = 4


def from_partner(block, axis, apart):
    count = lax.axis_size(axis)
    route = []
    for low in range(count):
        high = low | 1 << apart
        if high != low and high < count:
            route += [(low, high), (high, low)]
    return lax.ppermute(block, axis, route)


def slot_tables(routing_dev):
    flat_experts = routing_dev.reshape(-1)
    onehot = (flat_experts[:, None] == jnp.arange(EXPERTS, dtype=jnp.int32)[None, :]).astype(
        jnp.int32
    )
    before = jnp.cumsum(onehot, axis=0) - onehot
    slot_index = jnp.sum(before * onehot, axis=1)
    target = flat_experts * CAP + slot_index
    placed = target[:, None] == jnp.arange(EXPERTS * CAP, dtype=jnp.int32)[None, :]
    return placed.astype(jnp.float32)


def contract_rows(left_rows, right_rows):
    return lax.dot_general(
        left_rows, right_rows, (((0,), (0,)), ((), ())), preferred_element_type=jnp.float32
    )


def rounded(value):
    return lax.optimization_barrier(value.astype(jnp.bfloat16)).astype(jnp.float32)


def per_device(tokens, routing, hidden_grad, gate_weight, up_weight):
    token_count = tokens.shape[0]
    model_width = tokens.shape[1]
    ffd_cols = gate_weight.shape[1]
    shards = lax.axis_size("expert") // EXPERTS
    placed = slot_tables(routing)
    doubled = jnp.repeat(tokens, TOP, axis=0)
    outgoing = jnp.dot(
        placed.T.astype(jnp.bfloat16), doubled, preferred_element_type=jnp.float32
    ).astype(jnp.bfloat16)
    copies = jnp.broadcast_to(
        outgoing.reshape(EXPERTS, 1, CAP, model_width), (EXPERTS, shards, CAP, model_width)
    )
    copies = copies.reshape(EXPERTS * shards, CAP, model_width)
    arrived = lax.all_to_all(copies, "expert", split_axis=0, concat_axis=0, tiled=True)
    expert_rows = arrived.reshape(-1, model_width)
    gate_pre = jnp.dot(expert_rows, gate_weight, preferred_element_type=jnp.float32)
    up_pre = jnp.dot(expert_rows, up_weight, preferred_element_type=jnp.float32)
    grad_h = hidden_grad.astype(jnp.float32)
    sigmoid_gate = jax.nn.sigmoid(gate_pre)
    gate_grad = (grad_h * up_pre * sigmoid_gate * (1.0 + gate_pre * (1.0 - sigmoid_gate))).astype(
        jnp.bfloat16
    )
    up_grad = (grad_h * gate_pre * sigmoid_gate).astype(jnp.bfloat16)
    transposed = (((1,), (1,)), ((), ()))
    partial_value = lax.dot_general(
        gate_grad, gate_weight, transposed, preferred_element_type=jnp.float32
    )
    partial_value = partial_value + lax.dot_general(
        up_grad, up_weight, transposed, preferred_element_type=jnp.float32
    )
    partial_value = partial_value.astype(jnp.bfloat16)
    returned = lax.all_to_all(
        partial_value.reshape(-1, CAP, model_width),
        "expert",
        split_axis=0,
        concat_axis=0,
        tiled=True,
    )
    summed = jnp.sum(
        returned.astype(jnp.float32).reshape(EXPERTS, shards, CAP, model_width), axis=1
    )
    summed = summed.reshape(EXPERTS * CAP, model_width)
    gathered = jnp.dot(placed, summed)
    token_grad = jnp.sum(gathered.reshape(token_count, TOP, model_width), axis=1).astype(
        jnp.bfloat16
    )
    grads_pair = jnp.concatenate([gate_grad, up_grad], axis=1)
    half_width = model_width // lax.axis_size("dp")
    replica_index = lax.axis_index("dp")
    own_columns = lax.dynamic_slice_in_dim(expert_rows, replica_index * half_width, half_width, 1)
    far_columns = lax.dynamic_slice_in_dim(
        expert_rows, (1 - replica_index) * half_width, half_width, 1
    )
    their_columns = from_partner(far_columns, "dp", 0)
    their_grads = from_partner(grads_pair, "dp", 0)
    weight_sum = rounded(contract_rows(own_columns, grads_pair)) + rounded(
        contract_rows(their_columns, their_grads)
    )
    gate_weight_grad = weight_sum[:, :ffd_cols].astype(jnp.bfloat16)
    up_weight_grad = weight_sum[:, ffd_cols:].astype(jnp.bfloat16)
    return (token_grad, gate_weight_grad, up_weight_grad)


def solution(mesh):
    in_specs = (
        P(("dp", "expert"), None),
        P(("dp", "expert"), None),
        P(("dp", "expert"), None),
        P(None, "expert"),
        P(None, "expert"),
    )
    out_specs = (P(("dp", "expert"), None), P("dp", "expert"), P("dp", "expert"))
    return jax.shard_map(
        per_device, mesh=mesh, in_specs=in_specs, out_specs=out_specs, check_vma=False
    )
```

profile of v0, /device:TPU:16, one launch (start us, length us, event | category | flops | bytes accessed | tf_op | source)
XLA Modules:
  0.0 283.9 jit_solution(1764236458276852436)
XLA Ops:
  0.6 0.8 copy.18
  1.4 0.1 eq.51
  1.5 0.1 fusion.6
  1.5 0.1 reduce_window_sum.11
  1.6 0.2 select_reduce_fusion
  1.8 1.1 broadcast_in_dim.6
  2.9 0.1 reshape.64
  3.0 0.2 convolution_convert_fusion
  3.2 0.1 broadcast_in_dim.14
  3.3 4.0 %broadcast_in_dim.15 = bf16[8,16,4,4096]{3,2,1,0:T(4,128)(2,1)} broadcast(bf16[8,4,4096]{2,1,0:T(4,128)(2,1)S(1)} %broadcast_in_dim.14), dimensions={0,2,3} | broadcast | bytes 4456448 | tf_op jit(solution)/shard_map/broadcast_in_dim | solution.py:53
  7.4 0.0 copy-start.3
  7.4 14.7 %all-to-all-start = ((bf16[128,4,4096]{2,1,0:T(4,128)(2,1)}), bf16[128,4,4096]{2,1,0:T(4,128)(2,1)}, u32[]{:S(2)}, u32[]{:S(2)}) async-start(bf16[128,4,4096]{2,1,0:T(4,128)(2,1)} %bitcast.19), calls=%async_computation | async-start | bytes 8388608 | tf_op jit(solution)/shard_map/all_to_all | solution.py:57
  22.1 0.0 copy-done.3
  22.1 0.2 copy.20
  22.3 95.2 %all-to-all-done = bf16[128,4,4096]{2,1,0:T(4,128)(2,1)} async-done(((bf16[128,4,4096]{2,1,0:T(4,128)(2,1)}), bf16[128,4,4096]{2,1,0:T(4,128)(2,1)}, u32[]{:S(2)}, u32[]{:S(2)}) %all-to-all-start) | async-done | bytes 4194336 | tf_op jit(solution)/shard_map/all_to_all | solution.py:57
  117.6 6.9 %reshape.66 = bf16[512,4096]{1,0:T(8,128)(2,1)} reshape(bf16[128,4,4096]{2,1,0:T(4,128)(2,1)} %all-to-all-done) | data formatting | bytes 8388608 | tf_op jit(solution)/shard_map/reshape | solution.py:58
  124.5 0.0 copy-start
  124.5 0.0 copy-start.2
  124.5 6.1 %fusion.5 = (bf16[512,512]{0,1:T(8,128)(2,1)S(1)}, f32[512,512]{0,1:T(8,128)S(1)}) fusion(bf16[512,512]{0,1:T(8,128)(2,1)S(1)} %copy.20, bf16[512,4096]{1,0:T(8,128)(2,1)} %reshape.66, bf16[4096,512]{1,0:T(8,128)(2,1)} %param.8), kind=kOutput, calls=%fused_computation.14 | convolution fusion | flops 2149318656 | bytes 10485760 | tf_op jit(solution)/shard_map/dot_general | solution.py:59
  130.6 0.0 copy-done
  130.6 0.0 copy-done.2
  130.6 0.0 copy-start.1
  130.6 2.6 fusion.3
  133.2 0.0 copy-done.1
  133.3 2.4 fusion.13
  135.7 4.5 %add_convert_fusion.1 = bf16[512,4096]{1,0:T(8,128)(2,1)} fusion(f32[512,4096]{1,0:T(8,128)S(1)} %fusion.13, bf16[512,512]{0,1:T(8,128)(2,1)S(1)} %get-tuple-element.5, bf16[4096,512]{1,0:T(8,128)(2,1)S(1)} %copy-done.2), kind=kOutput, calls=%fused_computation.2 | convolution fusion | flops 2151677952 | bytes 17301504 | tf_op jit(solution)/shard_map/dot_general | solution.py:71
  140.2 7.2 %reshape.67 = bf16[128,4,4096]{2,1,0:T(4,128)(2,1)} reshape(bf16[512,4096]{1,0:T(8,128)(2,1)} %add_convert_fusion.1) | data formatting | bytes 8388608 | tf_op jit(solution)/shard_map/reshape | solution.py:76
  147.4 8.0 %all-to-all-start.1 = ((bf16[128,4,4096]{2,1,0:T(4,128)(2,1)}), bf16[128,4,4096]{2,1,0:T(4,128)(2,1)}, u32[]{:S(2)}, u32[]{:S(2)}) async-start(bf16[128,4,4096]{2,1,0:T(4,128)(2,1)} %reshape.67), calls=%async_computation.1 | async-start | bytes 8388608 | tf_op jit(solution)/shard_map/all_to_all | solution.py:75
  155.3 0.0 copy-start.4
  155.4 1.7 constant_dynamic-slice_fusion
  157.1 0.7 collective-permute-start
  157.8 1.0 pad_maximum_fusion
  158.8 2.9 %collective-permute-start.1 = (bf16[512,1024]{0,1:T(8,128)(2,1)}, bf16[512,1024]{0,1:T(8,128)(2,1)}, u32[]{:S(2)}, u32[]{:S(2)}) collective-permute-start(bf16[512,1024]{0,1:T(8,128)(2,1)} %pad_maximum_fusion), channel_id=1, source_target_pairs={{0,128},{128,0},{1,129},{129,1},{2,130},{130,2},{3,131},{131,3},{4... | collective-permute-start | bytes 3145736 | tf_op jit(solution)/shard_map/ppermute | solution.py:18
  161.7 0.1 reduce_sum.30
  161.8 0.1 copy.19
  161.9 0.0 copy-done.4
  161.9 4.0 %convolution_convert_fusion.2 = bf16[2048,1024]{1,0:T(8,128)(2,1)S(1)} fusion(bf16[512,4096]{1,0:T(8,128)(2,1)} %reshape.66, s32[]{:T(128)S(6)} %select_n.6, bf16[512,512]{0,1:T(8,128)(2,1)S(1)} %get-tuple-element.5, bf16[512,512]{0,1:T(8,128)(2,1)S(1)} %fusion.3), kind=kOutput, calls=%fused_computation.5 | convolution fusion | flops 2151677952 | bytes 7340036 | tf_op jit(solution)/shard_map/dot_general | solution.py:34
  165.9 103.7 %collective-permute-done.1 = bf16[512,1024]{0,1:T(8,128)(2,1)} collective-permute-done((bf16[512,1024]{0,1:T(8,128)(2,1)}, bf16[512,1024]{0,1:T(8,128)(2,1)}, u32[]{:S(2)}, u32[]{:S(2)}) %collective-permute-start.1) | collective-permute-done | bytes 1048608 | tf_op jit(solution)/shard_map/ppermute | solution.py:18
  269.7 0.0 collective-permute-done
  269.7 4.3 %convolution_convert_fusion.1 = bf16[2048,1024]{1,0:T(8,128)(2,1)S(1)} fusion(bf16[512,2048]{1,0:T(8,128)(2,1)} %collective-permute-done, bf16[512,1024]{0,1:T(8,128)(2,1)} %collective-permute-done.1), kind=kOutput, calls=%fused_computation.4 | convolution fusion | flops 2149580800 | bytes 7340032 | tf_op jit(solution)/shard_map/dot_general | solution.py:34
  273.9 2.2 add_convert_fusion
  276.2 2.3 fusion.12
  278.4 0.0 all-to-all-done.1
  278.4 4.4 %convert_reduce_fusion = bf16[8,4,4096]{2,1,0:T(4,128)(2,1)S(1)} fusion(bf16[128,4,4096]{2,1,0:T(4,128)(2,1)} %all-to-all-done.1), kind=kLoop, calls=%fused_computation | loop fusion | flops 4063232 | bytes 4456448 | tf_op jit(solution)/shard_map/reduce_sum | solution.py:82
  282.9 0.1 reshape.73
  282.9 0.9 convolution_reduce_fusion
  (2 shorter events, 0.0 us)
Async XLA Ops:
  7.4 14.7 %copy-start.3 = (bf16[512,512]{1,0:T(8,128)(2,1)S(1)}, bf16[512,512]{1,0:T(8,128)(2,1)}, u32[]{:S(2)}) copy-start(bf16[512,512]{1,0:T(8,128)(2,1)} %param.7) | copy-start | bytes 1572868
  7.4 110.2 %all-to-all-start = ((bf16[128,4,4096]{2,1,0:T(4,128)(2,1)}), bf16[128,4,4096]{2,1,0:T(4,128)(2,1)}, u32[]{:S(2)}, u32[]{:S(2)}) async-start(bf16[128,4,4096]{2,1,0:T(4,128)(2,1)} %bitcast.19), calls=%async_computation | async-start | bytes 8388608 | tf_op jit(solution)/shard_map/all_to_all | solution.py:57
  124.5 6.1 %copy-start = (bf16[512,4096]{1,0:T(8,128)(2,1)S(1)}, bf16[512,4096]{1,0:T(8,128)(2,1)}, u32[]{:S(2)}) copy-start(bf16[512,4096]{1,0:T(8,128)(2,1)} %reshape.66) | copy-start | bytes 12582916
  124.5 6.1 %copy-start.2 = (bf16[4096,512]{1,0:T(8,128)(2,1)S(1)}, bf16[4096,512]{1,0:T(8,128)(2,1)}, u32[]{:S(2)}) copy-start(bf16[4096,512]{1,0:T(8,128)(2,1)} %param.9) | copy-start | bytes 12582916
  130.6 2.6 copy-start.1
  147.4 131.1 %all-to-all-start.1 = ((bf16[128,4,4096]{2,1,0:T(4,128)(2,1)}), bf16[128,4,4096]{2,1,0:T(4,128)(2,1)}, u32[]{:S(2)}, u32[]{:S(2)}) async-start(bf16[128,4,4096]{2,1,0:T(4,128)(2,1)} %reshape.67), calls=%async_computation.1 | async-start | bytes 8388608 | tf_op jit(solution)/shard_map/all_to_all | solution.py:75
  155.3 6.6 %copy-start.4 = (s32[16,2]{0,1:T(2,128)S(1)}, s32[16,2]{0,1:T(2,128)}, u32[]{:S(2)}) copy-start(s32[16,2]{0,1:T(2,128)} %param.6) | copy-start | bytes 388
  157.1 112.6 %collective-permute-start = (bf16[512,2048]{1,0:T(8,128)(2,1)S(1)}, bf16[512,2048]{1,0:T(8,128)(2,1)}, u32[]{:S(2)}, u32[]{:S(2)}) collective-permute-start(bf16[512,2048]{1,0:T(8,128)(2,1)S(1)} %constant_dynamic-slice_fusion), channel_id=1, source_target_pairs={{0,128},{128,0},{1,129},{129,1},{2,130},{130,2},{3,131},{131,3},{4... | collective-permute-start | bytes 6291464 | tf_op jit(solution)/shard_map/ppermute | solution.py:18
  158.8 110.8 %collective-permute-start.1 = (bf16[512,1024]{0,1:T(8,128)(2,1)}, bf16[512,1024]{0,1:T(8,128)(2,1)}, u32[]{:S(2)}, u32[]{:S(2)}) collective-permute-start(bf16[512,1024]{0,1:T(8,128)(2,1)} %pad_maximum_fusion), channel_id=1, source_target_pairs={{0,128},{128,0},{1,129},{129,1},{2,130},{130,2},{3,131},{131,3},{4... | collective-permute-start | bytes 3145736 | tf_op jit(solution)/shard_map/ppermute | solution.py:18
where the time goes:
time: 287 us; the launch traced here: 284 us
  waiting for transfers between devices  199 us (69%)
  starting transfers between devices  26.3 us (9%)
  matrix products  25 us (9%)
  local copies, waits for them, and re-layouts  24.7 us (9%)
  other arithmetic  8 us (3%)
    ppermute x2, waiting for transfers between devices, from_partner(): return lax.ppermute(block, axis, route)  104 us
    all_to_all x1, waiting for transfers between devices, per_device(): lax.all_to_all(copies, 'expert', split_axis=0, concat_axis=0, tiled=True)  95.2 us
    all_to_all x1, starting transfers between devices, per_device(): lax.all_to_all(copies, 'expert', split_axis=0, concat_axis=0, tiled=True)  14.7 us
    dot_general x2, matrix products, contract_rows(): lax.dot_general(left_rows, right_rows, (((0,), (0,)), ((), ())), preferre...  8.26 us
    all_to_all x1, starting transfers between devices, per_device(): lax.all_to_all(partial_value.reshape(-1, CAP, model_width), 'expert', spl...  7.96 us
    reshape x1, local copies, waits for them, and re-layouts, per_device(): partial_value.reshape(-1, CAP, model_width)  7.2 us
    reshape x1, local copies, waits for them, and re-layouts, per_device(): expert_rows = arrived.reshape(-1, model_width)  6.89 us
    dot_general x1, matrix products, per_device(): jnp.dot(expert_rows, gate_weight, preferred_element_type=jnp.float32)  6.12 us
  transfers between devices with their start and end apart: 4, of which 2 were waited for; matrix products, arithmetic and copies ran while one was open for 6% of the time, Pallas kernels for 0%

commit v1 on v0

v1 whole, which is shorter than its diff:
```python
import jax
import jax.numpy as jnp
from jax import lax
from jax.sharding import Mesh, PartitionSpec as P

EXPERTS = 8
TOP = 2
CAP = 4


def slot_tables(routing_dev):
    flat_experts = routing_dev.reshape(-1)
    onehot = (flat_experts[:, None] == jnp.arange(EXPERTS, dtype=jnp.int32)[None, :]).astype(
        jnp.int32
    )
    before = jnp.cumsum(onehot, axis=0) - onehot
    slot_index = jnp.sum(before * onehot, axis=1)
    target = flat_experts * CAP + slot_index
    placed = target[:, None] == jnp.arange(EXPERTS * CAP, dtype=jnp.int32)[None, :]
    return placed.astype(jnp.float32)


def contract_rows(left_rows, right_rows):
    return lax.dot_general(
        left_rows, right_rows, (((0,), (0,)), ((), ())), preferred_element_type=jnp.float32
    )


def swap_dp(block):
    return lax.ppermute(block, "dp", [(0, 1), (1, 0)])


def per_device(tokens, routing, hidden_grad, gate_weight, up_weight):
    token_count, model_width = tokens.shape
    ffd = gate_weight.shape[1]
    shards = lax.axis_size("s")
    half = model_width // 2
    replica = lax.axis_index("dp")
    placed = slot_tables(routing)
    chosen = jnp.sum(placed.reshape(token_count, TOP, EXPERTS * CAP), axis=1)
    outgoing = lax.dot_general(
        chosen.astype(jnp.bfloat16), tokens, (((0,), (0,)), ((), ())),
        preferred_element_type=jnp.float32,
    ).astype(jnp.bfloat16)
    mine = lax.all_to_all(
        outgoing.reshape(EXPERTS, CAP, model_width), "e", split_axis=0, concat_axis=0, tiled=True
    ).reshape(EXPERTS * CAP, model_width)
    far_mine = swap_dp(lax.dynamic_slice_in_dim(mine, (1 - replica) * half, half, 1))
    rows = lax.all_gather(mine, "s", axis=0, tiled=True)
    far_rows = lax.all_gather(far_mine, "s", axis=0, tiled=True)
    grad_h = (
        hidden_grad.reshape(EXPERTS, shards, CAP, ffd)
        .transpose(1, 0, 2, 3)
        .reshape(-1, ffd)
        .astype(jnp.float32)
    )
    gate_pre = jnp.dot(rows, gate_weight, preferred_element_type=jnp.float32)
    up_pre = jnp.dot(rows, up_weight, preferred_element_type=jnp.float32)
    sig = jax.nn.sigmoid(gate_pre)
    gate_grad = (grad_h * up_pre * sig * (1.0 + gate_pre * (1.0 - sig))).astype(jnp.bfloat16)
    up_grad = (grad_h * gate_pre * sig).astype(jnp.bfloat16)
    grads = jnp.concatenate([gate_grad, up_grad], axis=1)
    far_grads = swap_dp(grads)
    transposed = (((1,), (1,)), ((), ()))
    partial_value = lax.dot_general(
        gate_grad, gate_weight, transposed, preferred_element_type=jnp.float32
    )
    partial_value = partial_value + lax.dot_general(
        up_grad, up_weight, transposed, preferred_element_type=jnp.float32
    )
    partial_value = partial_value.astype(jnp.bfloat16)
    summed = lax.psum_scatter(partial_value, "s", scatter_dimension=0, tiled=True)
    back = lax.all_to_all(
        summed.reshape(EXPERTS, CAP, model_width), "e", split_axis=0, concat_axis=0, tiled=True
    ).reshape(EXPERTS * CAP, model_width)
    token_grad = jnp.dot(
        chosen.astype(jnp.bfloat16), back, preferred_element_type=jnp.float32
    ).astype(jnp.bfloat16)
    own_columns = lax.dynamic_slice_in_dim(rows, replica * half, half, 1)
    own_term = lax.optimization_barrier(contract_rows(own_columns, grads).astype(jnp.bfloat16))
    weight_sum = own_term.astype(jnp.float32) + contract_rows(far_rows, far_grads)
    return (
        token_grad,
        weight_sum[:, :ffd].astype(jnp.bfloat16),
        weight_sum[:, ffd:].astype(jnp.bfloat16),
    )


def solution(mesh):
    n_dp, n_expert = mesh.devices.shape
    fine = Mesh(mesh.devices.reshape(n_dp, EXPERTS, n_expert // EXPERTS), ("dp", "e", "s"))
    all_axes = ("dp", "e", "s")
    in_specs = (
        P(all_axes, None),
        P(all_axes, None),
        P(all_axes, None),
        P(None, ("e", "s")),
        P(None, ("e", "s")),
    )
    out_specs = (P(all_axes, None), P("dp", ("e", "s")), P("dp", ("e", "s")))
    return jax.shard_map(
        per_device, mesh=fine, in_specs=in_specs, out_specs=out_specs, check_vma=False
    )
```

time: 287 us -> 192 us (0.67)
  waiting for transfers between devices: 199 us -> 116 us
  starting transfers between devices: 26.3 us -> 6.69 us
  between operations: 0.82 us -> 13.9 us
  local copies, waits for them, and re-layouts: 24.7 us -> 12 us
  blocking collectives: 0 us -> 12 us
  other arithmetic: 8 us -> 1.16 us
  matrix products: 25 us -> 29.9 us
    ppermute x2, waiting for transfers between devices: 104 us -> 8.23 us  [swap_dp(): return lax.ppermute(block, 'dp', [(0, 1), (1, 0)])]
    all_to_all x2 -> x1, waiting for transfers between devices: 95.2 us -> 2.43 us  [per_device(): lax.all_to_all(summed.reshape(EXPERTS, CAP, model_width), 'e', split_axis...]
    reduce_scatter x0 -> x1, waiting for transfers between devices: none -> 54.6 us  [per_device(): lax.psum_scatter(partial_value, 's', scatter_dimension=0, tiled=True)]
    all_gather x0 -> x2, waiting for transfers between devices: none -> 50.4 us  [the longest x1 32.5 us: per_device(): rows = lax.all_gather(mine, 's', axis=0, tiled=True)]
    all_to_all x2 -> x1, starting transfers between devices: 22.7 us -> 5.07 us  [per_device(): lax.all_to_all(summed.reshape(EXPERTS, CAP, model_width), 'e', split_axis...]
    all_to_all x0 -> x1, blocking collectives: none -> 12 us  [per_device(): lax.all_to_all(outgoing.reshape(EXPERTS, CAP, model_width), 'e', split_ax...]
    reshape x4, local copies, waits for them, and re-layouts: 14.3 us -> 2.7 us  [the longest x1 1.76 us: per_device(): summed.reshape(EXPERTS, CAP, model_width)]
    broadcast_in_dim x3 -> x0, local copies, waits for them, and re-layouts: 5.23 us -> none  [the longest x2 4.13 us: per_device(): jnp.broadcast_to(outgoing.reshape(EXPERTS, 1, CAP, model_width), (EXPERTS...]
  transfers between devices with their start and end apart: 4 -> 6, of which waited for: 2 -> 6; matrix products, arithmetic and copies ran while one was open for 6% -> 19% of each run, Pallas kernels for 0% -> 0%
where the time goes in v1:
time: 192 us; the launch traced here: 191 us
  waiting for transfers between devices  116 us (60%)
  matrix products  29.9 us (16%)
  between operations  13.9 us (7%)
  local copies, waits for them, and re-layouts  12 us (6%)
  blocking collectives  12 us (6%)
  starting transfers between devices  6.69 us (3%)
    reduce_scatter x1, waiting for transfers between devices, per_device(): lax.psum_scatter(partial_value, 's', scatter_dimension=0, tiled=True)  54.6 us
    all_gather x1, waiting for transfers between devices, per_device(): rows = lax.all_gather(mine, 's', axis=0, tiled=True)  32.5 us
    all_gather x1, waiting for transfers between devices, per_device(): far_rows = lax.all_gather(far_mine, 's', axis=0, tiled=True)  17.9 us
    dot_general x2, matrix products, contract_rows(): lax.dot_general(left_rows, right_rows, (((0,), (0,)), ((), ())), preferre...  13.2 us
    all_to_all x1, blocking collectives, per_device(): lax.all_to_all(outgoing.reshape(EXPERTS, CAP, model_width), 'e', split_ax...  12 us
    ppermute x2, waiting for transfers between devices, swap_dp(): return lax.ppermute(block, 'dp', [(0, 1), (1, 0)])  8.23 us
    dot_general x1, matrix products, per_device(): gate_pre = jnp.dot(rows, gate_weight, preferred_element_type=jnp.float32)  6.13 us
    all_to_all x1, starting transfers between devices, per_device(): lax.all_to_all(summed.reshape(EXPERTS, CAP, model_width), 'e', split_axis...  5.07 us
  transfers between devices with their start and end apart: 6, of which 6 were waited for; matrix products, arithmetic and copies ran while one was open for 19% of the time, Pallas kernels for 0%

profile of v1, /device:TPU:16, one launch (start us, length us, event | category | flops | bytes accessed | tf_op | source)
XLA Modules:
  0.0 191.4 jit_solution(17602063873971808503)
XLA Ops:
  7.2 0.0 copy-start
  7.2 0.0 all-gather.3.cloned.1.call-start
  7.2 0.8 copy.25
  8.0 0.1 eq.29
  8.1 0.1 fusion.4
  8.2 0.1 reduce_window_sum.11
  8.2 0.2 select_reduce_fusion
  8.4 0.1 reduce_sum.21
  8.5 0.1 copy.26
  8.6 0.7 multiply_add_fusion
  9.3 0.1 convert_reduce_fusion
  9.4 0.0 copy-done
  9.4 0.2 convolution_convert_fusion
  9.6 0.1 reshape.43
  9.7 12.0 %all_to_all.10 = bf16[8,4,4096]{2,1,0:T(4,128)(2,1)S(1)} all-to-all(bf16[8,4,4096]{2,1,0:T(4,128)(2,1)S(1)} %reshape.43), channel_id=1, replica_groups=mesh['dp'=2,'e'=8,'s'=16] {'e'}, dimensions={0} | all-to-all | bytes 524288 | tf_op jit(solution)/shard_map/all_to_all | solution.py:45
  21.8 0.8 reshape.44
  22.5 0.0 all-gather.3.cloned.1.call-update
  22.6 0.0 all-gather.5.cloned.1.call-start
  22.6 0.9 constant_dynamic-slice_fusion
  23.5 0.7 collective-permute-start
  24.2 5.8 %collective-permute-done = bf16[32,2048]{1,0:T(8,128)(2,1)S(1)} collective-permute-done((bf16[32,2048]{1,0:T(8,128)(2,1)S(1)}, bf16[32,2048]{1,0:T(8,128)(2,1)S(1)}, u32[]{:S(2)}, u32[]{:S(2)}) %collective-permute-start) | collective-permute-done | bytes 131104 | tf_op jit(solution)/shard_map/ppermute | solution.py:30
  30.1 0.7 copy-done.3
  30.7 0.0 all-gather.5.cloned.1.call-update
  30.8 0.0 reduce-scatter.2.cloned.1.call-start
  30.8 1.4 reshape.48
  32.2 0.1 copy.31
  32.3 0.4 reshape.47
  32.7 0.3 copy.28
  33.0 32.5 %all-gather.3.cloned.1.call-done = bf16[512,4096]{1,0:T(8,128)(2,1)} async-done(((bf16[32,4096]{1,0:T(8,128)(2,1)}), bf16[512,4096]{1,0:T(8,128)(2,1)}) %all-gather.3.cloned.1.call-update) | async-done | bytes 4194320 | tf_op jit(solution)/shard_map/all_gather | solution.py:49
  65.5 6.1 %multiply_convert_fusion = (bf16[512,512]{0,1:T(8,128)(2,1)S(1)}, f32[512,512]{0,1:T(8,128)S(1)}) fusion(f32[512,512]{0,1:T(8,128)S(1)} %copy.28, bf16[512,4096]{1,0:T(8,128)(2,1)} %all-gather.3.cloned.1.call-done, bf16[4096,512]{1,0:T(8,128)(2,1)} %param.8), kind=kOutput, calls=%fused_computation.12 | convolution fusion | flops 2149056512 | bytes 11010048 | tf_op jit(solution)/shard_map/dot_general | solution.py:57
  71.7 0.0 copy-start.1
  71.7 2.6 %fusion.3 = bf16[512,512]{0,1:T(8,128)(2,1)S(1)} fusion(f32[512,512]{0,1:T(8,128)S(1)} %copy.28, bf16[512,4096]{1,0:T(8,128)(2,1)S(1)} %copy-done.4, bf16[4096,512]{1,0:T(8,128)(2,1)S(1)} %copy-done.2, f32[512,512]{0,1:T(8,128)S(1)} %get-tuple-element.6), kind=kOutput, calls=%fused_computation.9 | convolution fusion | flops 2150105088 | bytes 11010048 | tf_op jit(solution)/shard_map/dot_general | solution.py:58
  74.3 2.4 %fusion.9 = f32[512,4096]{1,0:T(8,128)S(1)} fusion(bf16[512,512]{0,1:T(8,128)(2,1)S(1)} %fusion.3, bf16[4096,512]{1,0:T(8,128)(2,1)S(1)} %copy-done.1), kind=kOutput, calls=%fused_computation.25 | convolution fusion | flops 2147483648 | bytes 13107200 | tf_op jit(solution)/shard_map/dot_general | solution.py:65
  76.8 4.5 %add_convert_fusion.1 = bf16[512,4096]{1,0:T(8,128)(2,1)} fusion(f32[512,4096]{1,0:T(8,128)S(1)} %fusion.9, bf16[512,512]{0,1:T(8,128)(2,1)S(1)} %get-tuple-element.5, bf16[4096,512]{1,0:T(8,128)(2,1)S(1)} %copy-done.2), kind=kOutput, calls=%fused_computation.1 | convolution fusion | flops 2151677952 | bytes 17301504 | tf_op jit(solution)/shard_map/dot_general | solution.py:68
  81.2 0.0 reduce-scatter.2.cloned.1.call-update
  81.2 0.1 pad_maximum_fusion
  81.3 0.8 collective-permute-start.1
  82.1 6.0 %convolution_convert_fusion.2 = bf16[2048,1024]{1,0:T(8,128)(2,1)} fusion(bf16[512,4096]{1,0:T(8,128)(2,1)} %all-gather.3.cloned.1.call-done, s32[]{:T(128)S(6)} %select_n.6, bf16[512,512]{0,1:T(8,128)(2,1)S(1)} %get-tuple-element.5, bf16[512,512]{0,1:T(8,128)(2,1)S(1)} %fusion.3), kind=kOutput, calls=%fused_computation.4 | convolution fusion | flops 2151677952 | bytes 7340036 | tf_op jit(solution)/shard_map/dot_general | solution.py:24
  88.1 17.9 %all-gather.5.cloned.1.call-done = bf16[512,2048]{1,0:T(8,128)(2,1)} async-done(((bf16[32,2048]{1,0:T(8,128)(2,1)}), bf16[512,2048]{1,0:T(8,128)(2,1)}) %all-gather.5.cloned.1.call-update) | async-done | bytes 2097168 | tf_op jit(solution)/shard_map/all_gather | solution.py:50
  106.0 2.4 %collective-permute-done.1 = bf16[512,1024]{0,1:T(8,128)(2,1)S(1)} collective-permute-done((bf16[512,1024]{0,1:T(8,128)(2,1)S(1)}, bf16[512,1024]{0,1:T(8,128)(2,1)S(1)}, u32[]{:S(2)}, u32[]{:S(2)}) %collective-permute-start.1) | collective-permute-done | bytes 1048608 | tf_op jit(solution)/shard_map/ppermute | solution.py:30
  108.4 7.2 %add_convert_fusion = bf16[2048,1024]{1,0:T(8,128)(2,1)} fusion(bf16[2048,1024]{1,0:T(8,128)(2,1)} %convolution_convert_fusion.2, bf16[512,2048]{1,0:T(8,128)(2,1)} %all-gather.5.cloned.1.call-done, bf16[512,1024]{0,1:T(8,128)(2,1)S(1)} %collective-permute-done.1), kind=kOutput, calls=%fused_computation | convolution fusion | flops 2153775104 | bytes 11534336 | tf_op jit(solution)/shard_map/dot_general | solution.py:24
  115.6 54.6 %reduce-scatter.2.cloned.1.call-done = bf16[32,4096]{1,0:T(8,128)(2,1)} async-done(((bf16[512,4096]{1,0:T(8,128)(2,1)}), bf16[32,4096]{1,0:T(8,128)(2,1)}) %reduce-scatter.2.cloned.1.call-update) | async-done | bytes 262160 | tf_op jit(solution)/shard_map/reduce_scatter | solution.py:72
  170.2 1.8 reshape.45
  171.9 5.1 %all-to-all-start.1 = ((bf16[8,4,4096]{2,1,0:T(4,128)(2,1)}), bf16[8,4,4096]{2,1,0:T(4,128)(2,1)S(1)}, u32[]{:S(2)}, u32[]{:S(2)}) async-start(bf16[8,4,4096]{2,1,0:T(4,128)(2,1)} %reshape.45), calls=%async_computation.2 | async-start | bytes 524288 | tf_op jit(solution)/shard_map/all_to_all | solution.py:73
  177.0 4.5 %fusion.8 = (bf16[2048,512]{1,0:T(8,128)(2,1)}, bf16[2048,512]{1,0:T(8,128)(2,1)}) fusion(bf16[2048,1024]{1,0:T(8,128)(2,1)} %add_convert_fusion), kind=kLoop, calls=%fused_computation.24 | loop fusion | bytes 8388608 | tf_op jit(solution)/shard_map/slice | solution.py:85
  181.5 2.4 %all-to-all-done.1 = bf16[8,4,4096]{2,1,0:T(4,128)(2,1)S(1)} async-done(((bf16[8,4,4096]{2,1,0:T(4,128)(2,1)}), bf16[8,4,4096]{2,1,0:T(4,128)(2,1)S(1)}, u32[]{:S(2)}, u32[]{:S(2)}) %all-to-all-start.1) | async-done | bytes 262176 | tf_op jit(solution)/shard_map/all_to_all | solution.py:73
  183.9 0.1 reshape.46
  184.0 0.8 convolution_convert_fusion.1
  (6 shorter events, 0.0 us)
Async XLA Ops:
  7.2 2.2 %copy-start = (bf16[16,4096]{1,0:T(8,128)(2,1)S(1)}, bf16[16,4096]{1,0:T(8,128)(2,1)}, u32[]{:S(2)}) copy-start(bf16[16,4096]{1,0:T(8,128)(2,1)} %param.5) | copy-start | bytes 393220
  7.2 58.4 %all-gather.3.cloned.1.call-start = ((), (), s32[]{:S(2)}) async-start(), calls=%async_computation.3 | async-start | bytes 4456448 | tf_op jit(solution)/shard_map/all_gather | solution.py:49
  22.6 83.4 %all-gather.5.cloned.1.call-start = ((), (), s32[]{:S(2)}) async-start(), calls=%async_computation.5 | async-start | bytes 2228224 | tf_op jit(solution)/shard_map/all_gather | solution.py:50
  23.5 6.6 %collective-permute-start = (bf16[32,2048]{1,0:T(8,128)(2,1)S(1)}, bf16[32,2048]{1,0:T(8,128)(2,1)S(1)}, u32[]{:S(2)}, u32[]{:S(2)}) collective-permute-start(bf16[32,2048]{1,0:T(8,128)(2,1)S(1)} %constant_dynamic-slice_fusion), channel_id=1, source_target_pairs={{0,128},{128,0},{1,129},{129,1},{2,130},{130,2},{3,131},{131,3},{4... | collective-permute-start | bytes 393224 | tf_op jit(solution)/shard_map/ppermute | solution.py:30
  30.1 0.7 copy-start.3
  30.8 139.4 %reduce-scatter.2.cloned.1.call-start = ((), (), s32[]{:S(2)}) async-start(), calls=%async_computation.4 | async-start | bytes 4456448 | tf_op jit(solution)/shard_map/reduce_scatter | solution.py:72
  65.5 6.1 %copy-start.2 = (bf16[4096,512]{1,0:T(8,128)(2,1)S(1)}, bf16[4096,512]{1,0:T(8,128)(2,1)}, u32[]{:S(2)}) copy-start(bf16[4096,512]{1,0:T(8,128)(2,1)} %param.9) | copy-start | bytes 12582916
  65.5 6.2 %copy-start.4 = (bf16[512,4096]{1,0:T(8,128)(2,1)S(1)}, bf16[512,4096]{1,0:T(8,128)(2,1)}, u32[]{:S(2)}) copy-start(bf16[512,4096]{1,0:T(8,128)(2,1)} %all-gather.3.cloned.1.call-done) | copy-start | bytes 12582916
  71.7 2.6 %copy-start.1 = (bf16[4096,512]{1,0:T(8,128)(2,1)S(1)}, bf16[4096,512]{1,0:T(8,128)(2,1)}, u32[]{:S(2)}) copy-start(bf16[4096,512]{1,0:T(8,128)(2,1)} %param.8) | copy-start | bytes 12582916
  81.3 27.1 %collective-permute-start.1 = (bf16[512,1024]{0,1:T(8,128)(2,1)S(1)}, bf16[512,1024]{0,1:T(8,128)(2,1)S(1)}, u32[]{:S(2)}, u32[]{:S(2)}) collective-permute-start(bf16[512,1024]{0,1:T(8,128)(2,1)S(1)} %pad_maximum_fusion), channel_id=1, source_target_pairs={{0,128},{128,0},{1,129},{129,1},{2,130},{130,2},{3,131},{131,3},{4... | collective-permute-start | bytes 3145736 | tf_op jit(solution)/shard_map/ppermute | solution.py:30
  171.9 12.0 %all-to-all-start.1 = ((bf16[8,4,4096]{2,1,0:T(4,128)(2,1)}), bf16[8,4,4096]{2,1,0:T(4,128)(2,1)S(1)}, u32[]{:S(2)}, u32[]{:S(2)}) async-start(bf16[8,4,4096]{2,1,0:T(4,128)(2,1)} %reshape.45), calls=%async_computation.2 | async-start | bytes 524288 | tf_op jit(solution)/shard_map/all_to_all | solution.py:73
Sparse Core Ops, SparseCore 0:
  22.7 42.8 all-gather.2
  67.9 37.9 all-gather.4
  108.5 61.5 reduce-scatter.1
